TPU v7x, 32 devices: a whole 2x2x4 slice. The times are simulated.
32 devices in a mesh: ctx: 8 (over z, x), head: 4 (over y, core).
Axes of the slice: x: 2, y: 2, z: 4, core: 2. Of those that a mesh axis runs over, the one named last changes fastest.
Arguments:
- probe_vectors: bfloat16 [1024, 8192], P('ctx', 'head'), may hold values from -160 to 160
- lookup_tensor: bfloat16 [8192, 1024], P('ctx', 'head'), may hold values from -4.5 to 4.5
- payload_tensor: bfloat16 [8192, 1024], P('ctx', 'head'), may hold values from -6 to 6
- sequence_locations: int32 [1024], replicated, may hold values from 0 to 8191, as said below
- attention_return_matrix: bfloat16 [8192, 8192], P('head', 'ctx'), may hold values from -0.0625 to 0.0625
- skip_stream_state: bfloat16 [1024, 8192], P('head', 'ctx'), may hold values from -4 to 4
- early_rescaling_factor: float32 [8192], P('ctx'), may hold values from 0.5 to 1.5
- lexicon_projection_matrix: bfloat16 [8192, 65536], P(None, ('ctx', 'head')), may hold values from -0.1875 to 0.1875
- calibrating_divisor: float32 [1024], replicated, may hold values from 0.02 to 1
- desired_tokens_list: int32 [1024], replicated, may hold values from 0 to 65535
Outputs:
- hidden: bfloat16 [1024, 8192], P('head', 'ctx')
- logprob: float32 [1024], replicated
Inputs may be any that keep to these rules, and one draw needn't show every extreme that they name: `sequence_locations`: query i stands at a position from i * 8 to (i + 1) * 8 - 1; the last query stands at 8191.
All inputs are finite; a program needn't handle non-finite values.
Results may differ from a plain program's by a relative error of at most 0.0014.
The roundings to bfloat16 on the way count: a program that leaves them out, or rounds other values in their place, can miss the bound.
Values may be sent and summed in bfloat16 or wider, within the bound.
No kernel may reach another device: no remote copies, remote signals or barrier semaphores. Data moves between devices by JAX's collectives and lax.ppermute only.
A program may use at most 192 MiB of HBM per device.

v0:
```python
import jax
import jax.numpy as jnp
from jax import lax
from jax.sharding import PartitionSpec as P

D = 8192
QUERY_HEAD_COUNT = 64
KEY_VALUE_HEADS = 8
HEAD_SIZE = 128
neg_big = -1e30
eps = 1e-05


def local_attention(every_query, lookup_tensor, payload_tensor, sequence_locations, key_start):
    total_rows = every_query.shape[0]
    ctx_len = lookup_tensor.shape[0]
    kv_here = lookup_tensor.shape[1] // HEAD_SIZE
    group_size = QUERY_HEAD_COUNT // KEY_VALUE_HEADS
    scale_factor = HEAD_SIZE ** (-0.5)
    row_block = min(512, total_rows)
    query_heads = every_query.reshape(total_rows, kv_here, group_size, HEAD_SIZE)
    key_heads = lookup_tensor.reshape(ctx_len, kv_here, HEAD_SIZE)
    value_heads = payload_tensor.reshape(ctx_len, kv_here, HEAD_SIZE)
    key_pos = key_start + jnp.arange(ctx_len, dtype=jnp.int32)
    maxima, sums, accums = ([], [], [])
    for row_start in range(0, total_rows, row_block):
        row_pos = sequence_locations[row_start : row_start + row_block]
        visible = key_pos[None, None, :] <= row_pos[:, None, None]
        head_max, head_sum, head_acc = ([], [], [])
        for kv_head in range(kv_here):
            scores = (
                jnp.einsum(
                    "qhd,kd->qhk",
                    query_heads[row_start : row_start + row_block, kv_head],
                    key_heads[:, kv_head],
                    preferred_element_type=jnp.float32,
                )
                * scale_factor
            )
            block_max = jnp.max(jnp.where(visible, scores, neg_big), axis=-1)
            weights = jnp.where(visible, jnp.exp(scores - block_max[..., None]), 0.0)
            head_sum.append(jnp.sum(weights, axis=-1))
            head_max.append(block_max)
            head_acc.append(
                jnp.einsum(
                    "qhk,kd->qhd",
                    weights.astype(jnp.bfloat16),
                    value_heads[:, kv_head],
                    preferred_element_type=jnp.float32,
                )
            )
        maxima.append(jnp.concatenate(head_max, axis=1))
        sums.append(jnp.concatenate(head_sum, axis=1))
        accums.append(jnp.concatenate(head_acc, axis=1))
    return (
        jnp.concatenate(maxima, axis=0),
        jnp.concatenate(sums, axis=0),
        jnp.concatenate(accums, axis=0),
    )


def shards(
    probe_vectors,
    lookup_tensor,
    payload_tensor,
    sequence_locations,
    attention_return_matrix,
    skip_stream_state,
    early_rescaling_factor,
    lexicon_projection_matrix,
    calibrating_divisor,
    desired_tokens_list,
):
    heads_here = probe_vectors.shape[1] // HEAD_SIZE
    every_query = lax.all_gather(probe_vectors, "ctx", axis=0, tiled=True)
    key_start = lax.axis_index("ctx") * lookup_tensor.shape[0]
    local_max, local_sum, local_acc = local_attention(
        every_query, lookup_tensor, payload_tensor, sequence_locations, key_start
    )
    global_max = lax.pmax(local_max.astype(jnp.bfloat16), "ctx").astype(local_max.dtype)
    rescale = jnp.exp(local_max - global_max)
    acc_rows, sum_rows = (
        lax.psum_scatter(local_acc * rescale[..., None], "ctx", scatter_dimension=0, tiled=True),
        lax.psum_scatter(local_sum * rescale, "ctx", scatter_dimension=0, tiled=True),
    )
    attn = (
        (acc_rows / sum_rows[..., None])
        .astype(jnp.bfloat16)
        .reshape(acc_rows.shape[0], heads_here * HEAD_SIZE)
    )
    mixed_part = jnp.dot(
        lax.all_gather(attn, "ctx", axis=0, tiled=True),
        attention_return_matrix,
        preferred_element_type=jnp.float32,
    )
    mixed_rows = lax.psum_scatter(mixed_part, "head", scatter_dimension=0, tiled=True)
    hidden = (skip_stream_state.astype(jnp.float32) + mixed_rows).astype(jnp.bfloat16)
    widened = hidden.astype(jnp.float32)
    square_total = lax.psum(jnp.sum(widened * widened, axis=1), "ctx")
    normed = (
        widened * lax.rsqrt(square_total / D + eps)[:, None] * early_rescaling_factor[None, :]
    ).astype(jnp.bfloat16)
    full_rows = lax.all_gather(normed, "ctx", axis=1, tiled=True)
    early_class_energies = jnp.dot(
        lax.all_gather(full_rows, "head", axis=0, tiled=True),
        lexicon_projection_matrix,
        preferred_element_type=jnp.float32,
    )
    tempered_affinities = early_class_energies / calibrating_divisor[:, None]
    vocab_here = lexicon_projection_matrix.shape[1]
    offset = (lax.axis_index("ctx") * lax.axis_size("head") + lax.axis_index("head")) * vocab_here
    column_ids = jnp.arange(vocab_here, dtype=jnp.int32)[None, :] + offset
    picked = jnp.sum(
        jnp.where(column_ids == desired_tokens_list[:, None], tempered_affinities, 0.0), axis=1
    )
    local_peak = jnp.max(tempered_affinities, axis=1)
    peak = lax.pmax(local_peak, ("ctx", "head"))
    total, target_logit = lax.psum(
        (jnp.sum(jnp.exp(tempered_affinities - peak[:, None]), axis=1), picked), ("ctx", "head")
    )
    logprob = target_logit - peak - jnp.log(total)
    return (hidden, logprob)


def solution(mesh):
    placed = (
        P("ctx", "head"),
        P("ctx", "head"),
        P("ctx", "head"),
        P(),
        P("head", "ctx"),
        P("head", "ctx"),
        P("ctx"),
        P(None, ("ctx", "head")),
        P(),
        P(),
    )
    return jax.shard_map(
        shards, mesh=mesh, in_specs=placed, out_specs=(P("head", "ctx"), P()), check_vma=False
    )
```

profile of v0, /device:TPU:0, one launch (start us, length us, event | category | flops | bytes accessed | tf_op | source)
XLA Modules:
  0.0 878.8 jit_solution(8990251536320615546)
XLA Ops:
  7.2 0.0 all-gather.5.cloned.1.call-start
  7.2 2.0 copy.12
  9.3 0.0 all-gather.5.cloned.1.call-update
  9.3 0.0 reduce-scatter.6.cloned.1.call-start
  9.3 1.2 copy.14
  10.6 2.2 copy.16
  12.8 0.8 fusion.36
  13.6 0.7 broadcast_compare_fusion.1
  14.3 73.7 %all-gather.5.cloned.1.call-done = bf16[1024,2048]{0,1:T(8,128)(2,1)} async-done(((bf16[128,2048]{0,1:T(8,128)(2,1)}), bf16[1024,2048]{0,1:T(8,128)(2,1)}) %all-gather.5.cloned.1.call-update) | async-done | bytes 4194320 | tf_op jit(solution)/shard_map/all_gather | solution.py:75
  88.0 8.8 select_reduce_fusion.1
  96.8 15.3 %fusion.4 = (f32[512,8]{0,1:T(8,128)S(1)}, f32[512,8]{0,1:T(8,128)S(1)}, f32[512,8,1024]{2,0,1:T(8,128)}) fusion(f32[512,8,1024]{2,0,1:T(8,128)} %get-tuple-element.19, f32[512,8]{0,1:T(8,128)S(1)} %get-tuple-element.18, pred[512,1024]{1,0:T(8,128)(4,1)S(1)} %get-tuple-element.15, bf16[1024,2,128]{0,2,1:T(8,128)(2,1)S(1)} %bitcast.76, ...), kind=kOutput, calls=%fused_computation.12 | convolution fusion | flops 1103093760 | bytes 35438592 | tf_op jit(solution)/shard_map/qhd,kd->qhk/dot_general | solution.py:32
  112.1 7.6 fusion.10
  119.7 7.4 select_reduce_fusion.3
  127.1 14.7 %fusion = (f32[512,8]{0,1:T(8,128)S(1)}, f32[512,8]{0,1:T(8,128)S(1)}, f32[512,8,1024]{2,0,1:T(8,128)}) fusion(f32[512,8,1024]{2,0,1:T(8,128)} %get-tuple-element.22, f32[512,8]{0,1:T(8,128)S(1)} %get-tuple-element.21, pred[512,1024]{1,0:T(8,128)(4,1)S(1)} %get-tuple-element.14, bf16[1024,2,128]{0,2,1:T(8,128)(2,1)} %bitcast.77, ...), kind=kOutput, calls=%fused_computation.8 | convolution fusion | flops 1103093760 | bytes 35438592 | tf_op jit(solution)/shard_map/qhd,kd->qhk/dot_general | solution.py:32
  141.8 8.9 %fusion.14 = f32[512,8,128]{2,0,1:T(8,128)} fusion(f32[512,8,1024]{2,0,1:T(8,128)} %get-tuple-element.22, f32[512,8]{0,1:T(8,128)S(1)} %get-tuple-element.21, pred[512,1024]{1,0:T(8,128)(4,1)S(1)} %get-tuple-element.14, bf16[1024,2,128]{0,2,1:T(8,128)(2,1)} %bitcast.71), kind=kOutput, calls=%fused_computation.22 | convolution fusion | flops 1090519040 | bytes 19677184 | tf_op jit(solution)/shard_map/qhk,kd->qhd/dot_general | solution.py:45
  150.7 4.6 fusion.8
  155.3 8.5 fusion.12
  163.8 11.1 %fusion.2 = (f32[512,8]{0,1:T(8,128)S(1)}, f32[512,8]{0,1:T(8,128)S(1)}) fusion(f32[512,8,1024]{2,0,1:T(8,128)} %get-tuple-element.23, f32[512,8]{0,1:T(8,128)S(1)} %get-tuple-element.5, pred[512,1024]{1,0:T(8,128)(4,1)S(1)} %get-tuple-element.14, f32[512,8]{0,1:T(8,128)S(1)} %get-tuple-element.7, f32[512,8,1024]{2,0,1:T(8,128)S(1)} %bitcast.69, ...), kind=kLoop, calls=%fused_computation.10 | loop fusion | flops 33546240 | bytes 34668544 | tf_op jit(solution)/shard_map/reduce_sum | solution.py:42
  174.9 34.3 %pmax.14 = bf16[1024,16]{0,1:T(8,128)(2,1)S(1)} all-reduce(bf16[1024,16]{0,1:T(8,128)(2,1)S(1)} %fusion.27), channel_id=1, replica_groups=mesh['ctx'=8,'head'=4] {'ctx'}, use_global_device_ids=true, to_apply=%region_4.5 | all-reduce | flops 16384 | bytes 65536 | tf_op jit(solution)/shard_map/pmax | solution.py:80
  209.2 0.7 maximum_multiply_fusion.1
  209.8 0.0 reduce-scatter.6.cloned.1.call-update
  209.9 0.0 reduce-scatter.4.cloned.1.call-start
  209.9 8.0 maximum_multiply_fusion
  217.9 0.0 reduce-scatter.4.cloned.1.call-update
  218.0 0.0 all-gather.7.cloned.1.call-start
  218.0 44.1 %reduce-scatter.6.cloned.1.call-done = f32[128,16]{0,1:T(8,128)} async-done(((f32[1024,16]{0,1:T(8,128)}), f32[128,16]{0,1:T(8,128)}) %reduce-scatter.6.cloned.1.call-update) | async-done | bytes 8208 | tf_op jit(solution)/shard_map/reduce_scatter | solution.py:84
  262.1 150.6 %reduce-scatter.4.cloned.1.call-done = f32[128,16,128]{2,0,1:T(8,128)} async-done(((f32[1024,16,128]{2,0,1:T(8,128)}), f32[128,16,128]{2,0,1:T(8,128)}) %reduce-scatter.4.cloned.1.call-update) | async-done | bytes 1048592 | tf_op jit(solution)/shard_map/reduce_scatter | solution.py:83
  412.6 1.6 divide_convert_fusion
  414.2 1.0 copy.23
  415.2 0.0 all-gather.7.cloned.1.call-update
  415.3 0.3 reduce-scatter.8.cloned.1.call-start
  415.5 73.6 %all-gather.7.cloned.1.call-done = bf16[1024,2048]{0,1:T(8,128)(2,1)} async-done(((bf16[128,2048]{0,1:T(8,128)(2,1)}), bf16[1024,2048]{0,1:T(8,128)(2,1)}) %all-gather.7.cloned.1.call-update) | async-done | bytes 4194320 | tf_op jit(solution)/shard_map/all_gather | solution.py:92
  489.1 10.0 %fusion.38 = f32[1024,1024]{1,0:T(8,128)} fusion(bf16[1024,2048]{0,1:T(8,128)(2,1)} %all-gather.7.cloned.1.call-done, bf16[2048,1024]{1,0:T(8,128)(2,1)} %param.14), kind=kOutput, calls=%fused_computation.67 | convolution fusion | flops 4294967296 | bytes 12582912 | tf_op jit(solution)/shard_map/dot_general | solution.py:91
  499.1 0.0 reduce-scatter.8.cloned.1.call-update
  499.1 0.0 all-gather.9.cloned.1.call-start
  499.2 42.9 %reduce-scatter.8.cloned.1.call-done = f32[256,1024]{1,0:T(8,128)} async-done(((f32[1024,1024]{1,0:T(8,128)}), f32[256,1024]{1,0:T(8,128)}) %reduce-scatter.8.cloned.1.call-update) | async-done | bytes 1048592 | tf_op jit(solution)/shard_map/reduce_scatter | solution.py:96
  542.0 1.5 fusion.20
  543.5 21.4 %psum.21 = f32[256]{0:T(256)S(1)} all-reduce(f32[256]{0:T(256)S(1)} %get-tuple-element.10), channel_id=1, replica_groups=mesh['ctx'=8,'head'=4] {'ctx'}, use_global_device_ids=true, to_apply=%region_13.14 | all-reduce | flops 256 | bytes 2048 | tf_op jit(solution)/shard_map/psum | solution.py:99
  564.9 1.0 fusion.22
  565.9 0.0 all-gather.9.cloned.1.call-update
  565.9 0.0 all-gather.11.cloned.1.call-start
  566.0 69.2 %all-gather.9.cloned.1.call-done = bf16[256,8192]{1,0:T(8,128)(2,1)} async-done(((bf16[256,1024]{1,0:T(8,128)(2,1)}), bf16[256,8192]{1,0:T(8,128)(2,1)}) %all-gather.9.cloned.1.call-update) | async-done | bytes 4194320 | tf_op jit(solution)/shard_map/all_gather | solution.py:103
  635.2 106.0 %all-gather.11.cloned.1.call-done = bf16[1024,8192]{1,0:T(8,128)(2,1)} async-done(((bf16[256,8192]{1,0:T(8,128)(2,1)}), bf16[1024,8192]{1,0:T(8,128)(2,1)}) %all-gather.11.cloned.1.call-update) | async-done | bytes 16777232 | tf_op jit(solution)/shard_map/all_gather | solution.py:105
  741.2 45.0 %fusion.37 = (f32[1024]{0:T(1024)S(1)}, f32[1024,2048]{1,0:T(8,128)}) fusion(f32[1024]{0:T(1024)S(1)} %copy-done.9, bf16[1024,8192]{1,0:T(8,128)(2,1)} %all-gather.11.cloned.1.call-done, bf16[8192,2048]{1,0:T(8,128)(2,1)} %param.17), kind=kOutput, calls=%fused_computation.66 | convolution fusion | flops 34363932672 | bytes 58728448 | tf_op jit(solution)/shard_map/dot_general | solution.py:104
  786.2 39.5 %pmax.15 = f32[1024]{0:T(1024)S(1)} all-reduce(f32[1024]{0:T(1024)S(1)} %get-tuple-element.24), channel_id=1, replica_groups=mesh['ctx'=8,'head'=4] {'ctx','head'}, use_global_device_ids=true, to_apply=%region_17.18 | all-reduce | flops 1024 | bytes 8192 | tf_op jit(solution)/shard_map/pmax | solution.py:117
  825.6 4.7 select_reduce_fusion.4
  830.4 41.0 %all-reduce = (f32[1024]{0:T(1024)S(1)}, f32[1024]{0:T(1024)S(1)}) all-reduce(f32[1024]{0:T(1024)S(1)} %get-tuple-element.3, f32[1024]{0:T(1024)S(1)} %get-tuple-element.2), channel_id=1, replica_groups=mesh['ctx'=8,'head'=4] {'ctx','head'}, use_global_device_ids=true, to_apply=%region_19.20 | all-reduce | flops 2048 | bytes 16384 | tf_op jit(solution)/shard_map/psum | solution.py:118
  871.4 0.6 log_subtract_fusion
  (34 shorter events, 0.1 us)
Async XLA Ops:
  7.2 80.8 %all-gather.5.cloned.1.call-start = ((), (), s32[]{:S(2)}) async-start(), calls=%async_computation.3 | async-start | bytes 4718592 | tf_op jit(solution)/shard_map/all_gather | solution.py:75
  9.3 252.8 %reduce-scatter.6.cloned.1.call-start = ((), (), s32[]{:S(2)}) async-start(), calls=%async_computation.5 | async-start | bytes 73728 | tf_op jit(solution)/shard_map/reduce_scatter | solution.py:84
  10.6 101.5 %copy-start.3 = (bf16[1024,256]{0,1:T(8,128)(2,1)}, bf16[1024,256]{0,1:T(8,128)(2,1)S(1)}, u32[]{:S(2)}) copy-start(bf16[1024,256]{0,1:T(8,128)(2,1)S(1)} %copy.14) | copy-start | bytes 1572868
  88.0 8.8 copy-start.8
  96.8 15.3 %copy-start.1 = (bf16[1024,256]{0,1:T(8,128)(2,1)S(1)}, bf16[1024,256]{0,1:T(8,128)(2,1)}, u32[]{:S(2)}) copy-start(bf16[1024,256]{0,1:T(8,128)(2,1)} %copy.16) | copy-start | bytes 1572868
  112.1 7.6 copy-start.4
  127.1 23.5 %slice-start = ((s8[16777216]{0:T(1024)(128)(4,1)}), s8[4194304]{0:T(1024)(128)(4,1)S(1)}, s32[]{:S(2)}) async-start(s8[16777216]{0:T(1024)(128)(4,1)} %bitcast.68), calls=%async_computation.10 | async-start | bytes 8388608
  127.1 23.5 %slice-start.1 = ((s8[16777216]{0:T(1024)(128)(4,1)}), s8[4194304]{0:T(1024)(128)(4,1)S(1)}, s32[]{:S(2)}) async-start(s8[16777216]{0:T(1024)(128)(4,1)} %bitcast.68), calls=%async_computation.11 | async-start | bytes 8388608
  127.1 23.5 %slice-start.2 = ((s8[16777216]{0:T(1024)(128)(4,1)}), s8[4194304]{0:T(1024)(128)(4,1)S(1)}, s32[]{:S(2)}) async-start(s8[16777216]{0:T(1024)(128)(4,1)} %bitcast.68), calls=%async_computation.12 | async-start | bytes 8388608
  141.8 8.9 %slice-start.3 = ((s8[16777216]{0:T(1024)(128)(4,1)}), s8[4194304]{0:T(1024)(128)(4,1)S(1)}, s32[]{:S(2)}) async-start(s8[16777216]{0:T(1024)(128)(4,1)} %bitcast.68), calls=%async_computation.13 | async-start | bytes 8388608
  141.8 8.9 %copy-start.2 = (bf16[1024,256]{0,1:T(8,128)(2,1)S(1)}, bf16[1024,256]{0,1:T(8,128)(2,1)}, u32[]{:S(2)}) copy-start(bf16[1024,256]{0,1:T(8,128)(2,1)} %copy.16) | copy-start | bytes 1572868
  209.9 202.8 %reduce-scatter.4.cloned.1.call-start = ((), (), s32[]{:S(2)}) async-start(), calls=%async_computation.4 | async-start | bytes 9437184 | tf_op jit(solution)/shard_map/reduce_scatter | solution.py:83
  217.9 324.1 %copy-start.5 = (bf16[256,1024]{1,0:T(8,128)(2,1)S(1)}, bf16[256,1024]{1,0:T(8,128)(2,1)}, u32[]{:S(2)}) copy-start(bf16[256,1024]{1,0:T(8,128)(2,1)} %param.15) | copy-start | bytes 1572868
  218.0 346.9 %copy-start.7 = (f32[1024]{0:T(1024)S(1)}, f32[1024]{0:T(1024)}, u32[]{:S(2)}) copy-start(f32[1024]{0:T(1024)} %param.16) | copy-start | bytes 12292
  218.0 271.2 %all-gather.7.cloned.1.call-start = ((), (), s32[]{:S(2)}) async-start(), calls=%async_computation.6 | async-start | bytes 4718592 | tf_op jit(solution)/shard_map/all_gather | solution.py:92
  415.2 325.9 %copy-start.9 = (f32[1024]{0:T(1024)S(1)}, f32[1024]{0:T(1024)}, u32[]{:S(2)}) copy-start(f32[1024]{0:T(1024)} %param.18) | copy-start | bytes 12292
  415.3 126.8 %reduce-scatter.8.cloned.1.call-start = ((), (), s32[]{:S(2)}) async-start(), calls=%async_computation.7 | async-start | bytes 5242880 | tf_op jit(solution)/shard_map/reduce_scatter | solution.py:96
  499.1 136.0 %all-gather.9.cloned.1.call-start = ((), (), s32[]{:S(2)}) async-start(), calls=%async_computation.8 | async-start | bytes 4718592 | tf_op jit(solution)/shard_map/all_gather | solution.py:103
  543.5 242.7 %copy-start = (bf16[256,1024]{1,0:T(8,128)(2,1)}, bf16[256,1024]{1,0:T(8,128)(2,1)S(1)}, u32[]{:S(2)}) copy-start(bf16[256,1024]{1,0:T(8,128)(2,1)S(1)} %get-tuple-element.11) | copy-start | bytes 1572868
  565.9 175.3 %all-gather.11.cloned.1.call-start = ((), (), s32[]{:S(2)}) async-start(), calls=%async_computation.9 | async-start | bytes 20971520 | tf_op jit(solution)/shard_map/all_gather | solution.py:105
  635.2 190.4 %copy-start.6 = (s32[1024]{0:T(1024)S(1)}, s32[1024]{0:T(1024)}, u32[]{:S(2)}) copy-start(s32[1024]{0:T(1024)} %param.19) | copy-start | bytes 12292
Sparse Core Ops, SparseCore 0:
  10.6 77.3 all-gather.4
  210.0 52.0 reduce-scatter.5
  265.7 146.8 reduce-scatter.3
  415.4 73.7 all-gather.6
  499.2 42.7 reduce-scatter.7
  566.0 69.0 all-gather.8
  636.7 104.4 all-gather.10
where the time goes:
time: 879 us
  waiting for transfers between devices  560 us (64%)
  blocking collectives  136 us (15%)
  matrix products  131 us (15%)
  other arithmetic  29.8 us (3%)
  between operations  14.3 us (2%)
    reduce_scatter x1, waiting for transfers between devices, shards(): lax.psum_scatter(local_acc * rescale[..., None], 'ctx', scatter_dimension...  151 us
    all_gather x1, waiting for transfers between devices, shards(): lax.all_gather(full_rows, 'head', axis=0, tiled=True)  106 us
    all_gather x1, waiting for transfers between devices, shards(): every_query = lax.all_gather(probe_vectors, 'ctx', axis=0, tiled=True)  73.7 us
    all_gather x1, waiting for transfers between devices, shards(): lax.all_gather(attn, 'ctx', axis=0, tiled=True)  73.6 us
    all_gather x1, waiting for transfers between devices, shards(): full_rows = lax.all_gather(normed, 'ctx', axis=1, tiled=True)  69.2 us
    dot_general x4, matrix products, local_attention(): jnp.einsum('qhd,kd->qhk', query_heads[row_start:row_start + row_block, kv...  46.2 us
    dot_general x1, matrix products, shards(): jnp.dot(lax.all_gather(full_rows, 'head', axis=0, tiled=True), lexicon_pr...  45 us
    reduce_scatter x1, waiting for transfers between devices, shards(): lax.psum_scatter(local_sum * rescale, 'ctx', scatter_dimension=0, tiled=T...  44.1 us
  transfers between devices with their start and end apart: 7, of which 7 were waited for; matrix products, arithmetic and copies ran while one was open for 1% of the time, Pallas kernels for 0%

commit v1 on v0

--- a/solution.py
+++ b/solution.py
@@ -100,7 +100,12 @@
     normed = (
         widened * lax.rsqrt(square_total / D + eps)[:, None] * early_rescaling_factor[None, :]
     ).astype(jnp.bfloat16)
-    full_rows = lax.all_gather(normed, "ctx", axis=1, tiled=True)
+    ring = [normed]
+    for hop in range(7):
+        ring.append(lax.ppermute(ring[-1], "ctx", [(dev, (dev + 1) % 8) for dev in range(8)]))
+    full_rows = jnp.roll(
+        jnp.concatenate(ring[::-1], axis=1), (lax.axis_index("ctx") + 1) * ring[0].shape[1], axis=1
+    )
     early_class_energies = jnp.dot(
         lax.all_gather(full_rows, "head", axis=0, tiled=True),
         lexicon_projection_matrix,

time: 879 us -> 931 us (1.059)
  waiting for transfers between devices: 560 us -> 587 us
    ppermute x0 -> x7, waiting for transfers between devices: none -> 99.3 us  [shards(): lax.ppermute(ring[-1], 'ctx', [(dev, (dev + 1) % 8) for dev in range(8)])]
    all_gather x1 -> x0, waiting for transfers between devices: 69.2 us -> none  [shards(): full_rows = lax.all_gather(normed, 'ctx', axis=1, tiled=True)]
    dot_general x4, matrix products: 29.5 us -> 39.2 us  [local_attention(): jnp.einsum('qhk,kd->qhd', weights.astype(jnp.bfloat16), value_heads[:, kv...]
  transfers between devices with their start and end apart: 7 -> 13, of which waited for: 7 -> 13; matrix products, arithmetic and copies ran while one was open for 1% -> 1% of each run, Pallas kernels for 0% -> 0%
where the time goes in v1:
time: 931 us; the launch traced here: 922 us
  waiting for transfers between devices  587 us (63%)
  matrix products  140 us (15%)
  blocking collectives  136 us (15%)
  other arithmetic  29.3 us (3%)
  between operations  14.8 us (2%)
  local copies, waits for them, and re-layouts  14.2 us (2%)
    reduce_scatter x1, waiting for transfers between devices, shards(): lax.psum_scatter(local_acc * rescale[..., None], 'ctx', scatter_dimension...  151 us
    all_gather x1, waiting for transfers between devices, shards(): lax.all_gather(full_rows, 'head', axis=0, tiled=True)  102 us
    ppermute x7, waiting for transfers between devices, shards(): lax.ppermute(ring[-1], 'ctx', [(dev, (dev + 1) % 8) for dev in range(8)])  99.3 us
    all_gather x1, waiting for transfers between devices, shards(): lax.all_gather(attn, 'ctx', axis=0, tiled=True)  73.8 us
    all_gather x1, waiting for transfers between devices, shards(): every_query = lax.all_gather(probe_vectors, 'ctx', axis=0, tiled=True)  73.7 us
    dot_general x4, matrix products, local_attention(): jnp.einsum('qhd,kd->qhk', query_heads[row_start:row_start + row_block, kv...  46.2 us
    dot_general x1, matrix products, shards(): jnp.dot(lax.all_gather(full_rows, 'head', axis=0, tiled=True), lexicon_pr...  45 us
    reduce_scatter x1, waiting for transfers between devices, shards(): lax.psum_scatter(local_sum * rescale, 'ctx', scatter_dimension=0, tiled=T...  44 us
  transfers between devices with their start and end apart: 13, of which 13 were waited for; matrix products, arithmetic and copies ran while one was open for 1% of the time, Pallas kernels for 0%

profile of v1, /device:TPU:0, one launch (start us, length us, event | category | flops | bytes accessed | tf_op | source)
XLA Modules:
  0.0 921.8 jit_solution(4330356832637563184)
XLA Ops:
  7.2 2.0 copy.12
  9.3 1.2 copy.14
  10.6 2.2 copy.16
  12.8 0.8 fusion.36
  13.6 0.7 broadcast_compare_fusion.1
  14.3 73.7 %all-gather.4.cloned.1.call-done = bf16[1024,2048]{0,1:T(8,128)(2,1)} async-done(((bf16[128,2048]{0,1:T(8,128)(2,1)}), bf16[1024,2048]{0,1:T(8,128)(2,1)}) %all-gather.4.cloned.1.call-update) | async-done | bytes 4194320 | tf_op jit(solution)/shard_map/all_gather | solution.py:75
  88.0 8.8 select_reduce_fusion.1
  96.8 15.3 %fusion.4 = (f32[512,8]{0,1:T(8,128)S(1)}, f32[512,8]{0,1:T(8,128)S(1)}, f32[512,8,1024]{2,0,1:T(8,128)}) fusion(f32[512,8,1024]{2,0,1:T(8,128)} %get-tuple-element.19, f32[512,8]{0,1:T(8,128)S(1)} %get-tuple-element.18, pred[512,1024]{1,0:T(8,128)(4,1)S(1)} %get-tuple-element.15, bf16[1024,2,128]{0,2,1:T(8,128)(2,1)S(1)} %bitcast.76, ...), kind=kOutput, calls=%fused_computation.12 | convolution fusion | flops 1103093760 | bytes 35438592 | tf_op jit(solution)/shard_map/qhd,kd->qhk/dot_general | solution.py:32
  112.1 7.6 fusion.10
  119.7 7.4 select_reduce_fusion.3
  127.1 14.7 %fusion = (f32[512,8]{0,1:T(8,128)S(1)}, f32[512,8]{0,1:T(8,128)S(1)}, f32[512,8,1024]{2,0,1:T(8,128)}) fusion(f32[512,8,1024]{2,0,1:T(8,128)} %get-tuple-element.22, f32[512,8]{0,1:T(8,128)S(1)} %get-tuple-element.21, pred[512,1024]{1,0:T(8,128)(4,1)S(1)} %get-tuple-element.14, bf16[1024,2,128]{0,2,1:T(8,128)(2,1)} %bitcast.77, ...), kind=kOutput, calls=%fused_computation.8 | convolution fusion | flops 1103093760 | bytes 35438592 | tf_op jit(solution)/shard_map/qhd,kd->qhk/dot_general | solution.py:32
  141.8 18.5 %fusion.14 = f32[512,8,128]{2,0,1:T(8,128)} fusion(f32[512,8,1024]{2,0,1:T(8,128)} %get-tuple-element.22, f32[512,8]{0,1:T(8,128)S(1)} %get-tuple-element.21, pred[512,1024]{1,0:T(8,128)(4,1)S(1)} %get-tuple-element.14, bf16[1024,2,128]{0,2,1:T(8,128)(2,1)} %bitcast.71), kind=kOutput, calls=%fused_computation.22 | convolution fusion | flops 1090519040 | bytes 19677184 | tf_op jit(solution)/shard_map/qhk,kd->qhd/dot_general | solution.py:45
  160.4 4.6 fusion.8
  165.0 8.5 fusion.12
  173.4 11.1 %fusion.2 = (f32[512,8]{0,1:T(8,128)S(1)}, f32[512,8]{0,1:T(8,128)S(1)}) fusion(f32[512,8,1024]{2,0,1:T(8,128)} %get-tuple-element.23, f32[512,8]{0,1:T(8,128)S(1)} %get-tuple-element.5, pred[512,1024]{1,0:T(8,128)(4,1)S(1)} %get-tuple-element.14, f32[512,8]{0,1:T(8,128)S(1)} %get-tuple-element.7, f32[512,8,1024]{2,0,1:T(8,128)S(1)} %bitcast.69, ...), kind=kLoop, calls=%fused_computation.10 | loop fusion | flops 33546240 | bytes 34668544 | tf_op jit(solution)/shard_map/reduce_sum | solution.py:42
  184.5 34.3 %pmax.14 = bf16[1024,16]{0,1:T(8,128)(2,1)S(1)} all-reduce(bf16[1024,16]{0,1:T(8,128)(2,1)S(1)} %fusion.27), channel_id=1, replica_groups=mesh['ctx'=8,'head'=4] {'ctx'}, use_global_device_ids=true, to_apply=%region_4.5 | all-reduce | flops 16384 | bytes 65536 | tf_op jit(solution)/shard_map/pmax | solution.py:80
  218.9 0.7 maximum_multiply_fusion.1
  219.6 8.0 maximum_multiply_fusion
  227.7 44.0 %reduce-scatter.6.cloned.1.call-done = f32[128,16]{0,1:T(8,128)} async-done(((f32[1024,16]{0,1:T(8,128)}), f32[128,16]{0,1:T(8,128)}) %reduce-scatter.6.cloned.1.call-update) | async-done | bytes 8208 | tf_op jit(solution)/shard_map/reduce_scatter | solution.py:84
  271.7 150.6 %reduce-scatter.4.cloned.1.call-done = f32[128,16,128]{2,0,1:T(8,128)} async-done(((f32[1024,16,128]{2,0,1:T(8,128)}), f32[128,16,128]{2,0,1:T(8,128)}) %reduce-scatter.4.cloned.1.call-update) | async-done | bytes 1048592 | tf_op jit(solution)/shard_map/reduce_scatter | solution.py:83
  422.3 1.6 divide_convert_fusion
  423.8 1.0 copy.23
  425.0 73.8 %all-gather.6.cloned.1.call-done = bf16[1024,2048]{0,1:T(8,128)(2,1)} async-done(((bf16[128,2048]{0,1:T(8,128)(2,1)}), bf16[1024,2048]{0,1:T(8,128)(2,1)}) %all-gather.6.cloned.1.call-update) | async-done | bytes 4194320 | tf_op jit(solution)/shard_map/all_gather | solution.py:92
  498.8 10.0 %fusion.38 = f32[1024,1024]{1,0:T(8,128)} fusion(bf16[1024,2048]{0,1:T(8,128)(2,1)} %all-gather.6.cloned.1.call-done, bf16[2048,1024]{1,0:T(8,128)(2,1)} %param.14), kind=kOutput, calls=%fused_computation.84 | convolution fusion | flops 4294967296 | bytes 12582912 | tf_op jit(solution)/shard_map/dot_general | solution.py:91
  508.8 42.9 %reduce-scatter.8.cloned.1.call-done = f32[256,1024]{1,0:T(8,128)} async-done(((f32[1024,1024]{1,0:T(8,128)}), f32[256,1024]{1,0:T(8,128)}) %reduce-scatter.8.cloned.1.call-update) | async-done | bytes 1048592 | tf_op jit(solution)/shard_map/reduce_scatter | solution.py:96
  551.6 1.5 fusion.20
  553.1 21.4 %psum.21 = f32[256]{0:T(256)S(1)} all-reduce(f32[256]{0:T(256)S(1)} %get-tuple-element.10), channel_id=1, replica_groups=mesh['ctx'=8,'head'=4] {'ctx'}, use_global_device_ids=true, to_apply=%region_13.14 | all-reduce | flops 256 | bytes 2048 | tf_op jit(solution)/shard_map/psum | solution.py:99
  574.5 0.2 fusion.22
  574.8 12.4 %collective-permute-done = bf16[256,1024]{1,0:T(8,128)(2,1)S(1)} collective-permute-done((bf16[256,1024]{1,0:T(8,128)(2,1)S(1)}, bf16[256,1024]{1,0:T(8,128)(2,1)S(1)}, u32[]{:S(2)}, u32[]{:S(2)}) %collective-permute-start) | collective-permute-done | bytes 524320 | tf_op jit(solution)/shard_map/ppermute | solution.py:105
  587.2 12.7 %collective-permute-done.1 = bf16[256,1024]{1,0:T(8,128)(2,1)S(1)} collective-permute-done((bf16[256,1024]{1,0:T(8,128)(2,1)S(1)}, bf16[256,1024]{1,0:T(8,128)(2,1)S(1)}, u32[]{:S(2)}, u32[]{:S(2)}) %collective-permute-start.1) | collective-permute-done | bytes 524320 | tf_op jit(solution)/shard_map/ppermute | solution.py:105
  599.9 13.8 %collective-permute-done.2 = bf16[256,1024]{1,0:T(8,128)(2,1)S(1)} collective-permute-done((bf16[256,1024]{1,0:T(8,128)(2,1)S(1)}, bf16[256,1024]{1,0:T(8,128)(2,1)S(1)}, u32[]{:S(2)}, u32[]{:S(2)}) %collective-permute-start.2) | collective-permute-done | bytes 524320 | tf_op jit(solution)/shard_map/ppermute | solution.py:105
  613.7 15.0 %collective-permute-done.3 = bf16[256,1024]{1,0:T(8,128)(2,1)S(1)} collective-permute-done((bf16[256,1024]{1,0:T(8,128)(2,1)S(1)}, bf16[256,1024]{1,0:T(8,128)(2,1)S(1)}, u32[]{:S(2)}, u32[]{:S(2)}) %collective-permute-start.3) | collective-permute-done | bytes 524320 | tf_op jit(solution)/shard_map/ppermute | solution.py:105
  628.7 16.1 %collective-permute-done.4 = bf16[256,1024]{1,0:T(8,128)(2,1)S(1)} collective-permute-done((bf16[256,1024]{1,0:T(8,128)(2,1)S(1)}, bf16[256,1024]{1,0:T(8,128)(2,1)S(1)}, u32[]{:S(2)}, u32[]{:S(2)}) %collective-permute-start.4) | collective-permute-done | bytes 524320 | tf_op jit(solution)/shard_map/ppermute | solution.py:105
  644.8 17.1 %collective-permute-done.5 = bf16[256,1024]{1,0:T(8,128)(2,1)} collective-permute-done((bf16[256,1024]{1,0:T(8,128)(2,1)S(1)}, bf16[256,1024]{1,0:T(8,128)(2,1)}, u32[]{:S(2)}, u32[]{:S(2)}) %collective-permute-start.5) | collective-permute-done | bytes 524320 | tf_op jit(solution)/shard_map/ppermute | solution.py:105
  661.9 12.2 %collective-permute-done.6 = bf16[256,1024]{1,0:T(8,128)(2,1)} collective-permute-done((bf16[256,1024]{1,0:T(8,128)(2,1)}, bf16[256,1024]{1,0:T(8,128)(2,1)}, u32[]{:S(2)}, u32[]{:S(2)}) %collective-permute-start.6) | collective-permute-done | bytes 524320 | tf_op jit(solution)/shard_map/ppermute | solution.py:105
  674.1 1.1 constant_dynamic-update-slice_fusion.15
  675.2 1.1 constant_dynamic-update-slice_fusion.14
  676.5 0.2 constant_dynamic-update-slice_fusion.8
  676.7 1.1 constant_dynamic-update-slice_fusion.7
  677.8 1.1 constant_dynamic-update-slice_fusion.6
  679.1 0.2 constant_dynamic-update-slice_fusion
  679.3 2.2 constant_dynamic-slice_fusion
  681.5 102.4 %all-gather.8.cloned.1.call-done = bf16[1024,8192]{1,0:T(8,128)(2,1)} async-done(((bf16[256,8192]{1,0:T(8,128)(2,1)}), bf16[1024,8192]{1,0:T(8,128)(2,1)}) %all-gather.8.cloned.1.call-update) | async-done | bytes 16777232 | tf_op jit(solution)/shard_map/all_gather | solution.py:110
  784.0 45.0 %fusion.37 = (f32[1024]{0:T(1024)S(1)}, f32[1024,2048]{1,0:T(8,128)}) fusion(f32[1024]{0:T(1024)S(1)} %copy-done.9, bf16[1024,8192]{1,0:T(8,128)(2,1)} %all-gather.8.cloned.1.call-done, bf16[8192,2048]{1,0:T(8,128)(2,1)} %param.17), kind=kOutput, calls=%fused_computation.83 | convolution fusion | flops 34363932672 | bytes 58728448 | tf_op jit(solution)/shard_map/dot_general | solution.py:109
  828.9 39.3 %pmax.15 = f32[1024]{0:T(1024)S(1)} all-reduce(f32[1024]{0:T(1024)S(1)} %get-tuple-element.24), channel_id=1, replica_groups=mesh['ctx'=8,'head'=4] {'ctx','head'}, use_global_device_ids=true, to_apply=%region_17.18 | all-reduce | flops 1024 | bytes 8192 | tf_op jit(solution)/shard_map/pmax | solution.py:122
  868.2 4.7 select_reduce_fusion.4
  873.0 41.0 %all-reduce = (f32[1024]{0:T(1024)S(1)}, f32[1024]{0:T(1024)S(1)}) all-reduce(f32[1024]{0:T(1024)S(1)} %get-tuple-element.3, f32[1024]{0:T(1024)S(1)} %get-tuple-element.2), channel_id=1, replica_groups=mesh['ctx'=8,'head'=4] {'ctx','head'}, use_global_device_ids=true, to_apply=%region_19.20 | all-reduce | flops 2048 | bytes 16384 | tf_op jit(solution)/shard_map/psum | solution.py:123
  914.0 0.6 log_subtract_fusion
  (62 shorter events, 0.9 us)
Async XLA Ops:
  7.2 80.8 %all-gather.4.cloned.1.call-start = ((), (), s32[]{:S(2)}) async-start(), calls=%async_computation.3 | async-start | bytes 4718592 | tf_op jit(solution)/shard_map/all_gather | solution.py:75
  9.3 262.4 %reduce-scatter.6.cloned.1.call-start = ((), (), s32[]{:S(2)}) async-start(), calls=%async_computation.5 | async-start | bytes 73728 | tf_op jit(solution)/shard_map/reduce_scatter | solution.py:84
  10.6 86.2 %copy-start.3 = (bf16[1024,256]{0,1:T(8,128)(2,1)}, bf16[1024,256]{0,1:T(8,128)(2,1)S(1)}, u32[]{:S(2)}) copy-start(bf16[1024,256]{0,1:T(8,128)(2,1)S(1)} %copy.14) | copy-start | bytes 1572868
  88.0 8.8 copy-start.8
  96.8 15.3 %copy-start.1 = (bf16[1024,256]{0,1:T(8,128)(2,1)S(1)}, bf16[1024,256]{0,1:T(8,128)(2,1)}, u32[]{:S(2)}) copy-start(bf16[1024,256]{0,1:T(8,128)(2,1)} %copy.16) | copy-start | bytes 1572868
  112.1 7.6 copy-start.4
  127.1 33.2 %slice-start = ((s8[16777216]{0:T(1024)(128)(4,1)}), s8[4194304]{0:T(1024)(128)(4,1)S(1)}, s32[]{:S(2)}) async-start(s8[16777216]{0:T(1024)(128)(4,1)} %bitcast.68), calls=%async_computation.9 | async-start | bytes 8388608
  127.1 33.2 %slice-start.1 = ((s8[16777216]{0:T(1024)(128)(4,1)}), s8[4194304]{0:T(1024)(128)(4,1)S(1)}, s32[]{:S(2)}) async-start(s8[16777216]{0:T(1024)(128)(4,1)} %bitcast.68), calls=%async_computation.10 | async-start | bytes 8388608
  127.1 33.2 %slice-start.2 = ((s8[16777216]{0:T(1024)(128)(4,1)}), s8[4194304]{0:T(1024)(128)(4,1)S(1)}, s32[]{:S(2)}) async-start(s8[16777216]{0:T(1024)(128)(4,1)} %bitcast.68), calls=%async_computation.11 | async-start | bytes 8388608
  141.8 18.6 %slice-start.3 = ((s8[16777216]{0:T(1024)(128)(4,1)}), s8[4194304]{0:T(1024)(128)(4,1)S(1)}, s32[]{:S(2)}) async-start(s8[16777216]{0:T(1024)(128)(4,1)} %bitcast.68), calls=%async_computation.12 | async-start | bytes 8388608
  141.8 18.6 %copy-start.2 = (bf16[1024,256]{0,1:T(8,128)(2,1)S(1)}, bf16[1024,256]{0,1:T(8,128)(2,1)}, u32[]{:S(2)}) copy-start(bf16[1024,256]{0,1:T(8,128)(2,1)} %copy.16) | copy-start | bytes 1572868
  219.6 202.7 %reduce-scatter.4.cloned.1.call-start = ((), (), s32[]{:S(2)}) async-start(), calls=%async_computation.4 | async-start | bytes 9437184 | tf_op jit(solution)/shard_map/reduce_scatter | solution.py:83
  227.6 271.1 %all-gather.6.cloned.1.call-start = ((), (), s32[]{:S(2)}) async-start(), calls=%async_computation.6 | async-start | bytes 4718592 | tf_op jit(solution)/shard_map/all_gather | solution.py:92
  424.9 126.8 %copy-start.5 = (bf16[256,1024]{1,0:T(8,128)(2,1)S(1)}, bf16[256,1024]{1,0:T(8,128)(2,1)}, u32[]{:S(2)}) copy-start(bf16[256,1024]{1,0:T(8,128)(2,1)} %param.15) | copy-start | bytes 1572868
  424.9 149.6 %copy-start.6 = (f32[1024]{0:T(1024)S(1)}, f32[1024]{0:T(1024)}, u32[]{:S(2)}) copy-start(f32[1024]{0:T(1024)} %param.16) | copy-start | bytes 12292
  424.9 126.7 %reduce-scatter.8.cloned.1.call-start = ((), (), s32[]{:S(2)}) async-start(), calls=%async_computation.7 | async-start | bytes 5242880 | tf_op jit(solution)/shard_map/reduce_scatter | solution.py:96
  508.7 275.2 %all-gather.8.cloned.1.call-start = ((), (), s32[]{:S(2)}) async-start(), calls=%async_computation.8 | async-start | bytes 20971520 | tf_op jit(solution)/shard_map/all_gather | solution.py:110
  553.1 126.0 %copy-start = (bf16[256,1024]{1,0:T(8,128)(2,1)}, bf16[256,1024]{1,0:T(8,128)(2,1)S(1)}, u32[]{:S(2)}) copy-start(bf16[256,1024]{1,0:T(8,128)(2,1)S(1)} %get-tuple-element.11) | copy-start | bytes 1572868
  574.7 12.5 %collective-permute-start = (bf16[256,1024]{1,0:T(8,128)(2,1)S(1)}, bf16[256,1024]{1,0:T(8,128)(2,1)S(1)}, u32[]{:S(2)}, u32[]{:S(2)}) collective-permute-start(bf16[256,1024]{1,0:T(8,128)(2,1)S(1)} %fusion.22), channel_id=1, source_target_pairs={{0,4},{4,8},{8,12},{12,16},{16,20},{20,24},{24,28},{28,0},{1,5},{5... | collective-permute-start | bytes 1572872 | tf_op jit(solution)/shard_map/ppermute | solution.py:105
  587.2 12.7 %collective-permute-start.1 = (bf16[256,1024]{1,0:T(8,128)(2,1)S(1)}, bf16[256,1024]{1,0:T(8,128)(2,1)S(1)}, u32[]{:S(2)}, u32[]{:S(2)}) collective-permute-start(bf16[256,1024]{1,0:T(8,128)(2,1)S(1)} %collective-permute-done), channel_id=1, source_target_pairs={{0,4},{4,8},{8,12},{12,16},{16,20},{20,24},{24,28},{28,0},{1,5},{5... | collective-permute-start | bytes 1572872 | tf_op jit(solution)/shard_map/ppermute | solution.py:105
  599.9 13.8 %collective-permute-start.2 = (bf16[256,1024]{1,0:T(8,128)(2,1)S(1)}, bf16[256,1024]{1,0:T(8,128)(2,1)S(1)}, u32[]{:S(2)}, u32[]{:S(2)}) collective-permute-start(bf16[256,1024]{1,0:T(8,128)(2,1)S(1)} %collective-permute-done.1), channel_id=1, source_target_pairs={{0,4},{4,8},{8,12},{12,16},{16,20},{20,24},{24,28},{28,0},{1,5},{5... | collective-permute-start | bytes 1572872 | tf_op jit(solution)/shard_map/ppermute | solution.py:105
  613.7 15.0 %collective-permute-start.3 = (bf16[256,1024]{1,0:T(8,128)(2,1)S(1)}, bf16[256,1024]{1,0:T(8,128)(2,1)S(1)}, u32[]{:S(2)}, u32[]{:S(2)}) collective-permute-start(bf16[256,1024]{1,0:T(8,128)(2,1)S(1)} %collective-permute-done.2), channel_id=1, source_target_pairs={{0,4},{4,8},{8,12},{12,16},{16,20},{20,24},{24,28},{28,0},{1,5},{5... | collective-permute-start | bytes 1572872 | tf_op jit(solution)/shard_map/ppermute | solution.py:105
  628.7 16.1 %collective-permute-start.4 = (bf16[256,1024]{1,0:T(8,128)(2,1)S(1)}, bf16[256,1024]{1,0:T(8,128)(2,1)S(1)}, u32[]{:S(2)}, u32[]{:S(2)}) collective-permute-start(bf16[256,1024]{1,0:T(8,128)(2,1)S(1)} %collective-permute-done.3), channel_id=1, source_target_pairs={{0,4},{4,8},{8,12},{12,16},{16,20},{20,24},{24,28},{28,0},{1,5},{5... | collective-permute-start | bytes 1572872 | tf_op jit(solution)/shard_map/ppermute | solution.py:105
  644.8 17.1 %collective-permute-start.5 = (bf16[256,1024]{1,0:T(8,128)(2,1)S(1)}, bf16[256,1024]{1,0:T(8,128)(2,1)}, u32[]{:S(2)}, u32[]{:S(2)}) collective-permute-start(bf16[256,1024]{1,0:T(8,128)(2,1)S(1)} %collective-permute-done.4), channel_id=1, source_target_pairs={{0,4},{4,8},{8,12},{12,16},{16,20},{20,24},{24,28},{28,0},{1,5},{5... | collective-permute-start | bytes 1572872 | tf_op jit(solution)/shard_map/ppermute | solution.py:105
  661.9 12.2 %collective-permute-start.6 = (bf16[256,1024]{1,0:T(8,128)(2,1)}, bf16[256,1024]{1,0:T(8,128)(2,1)}, u32[]{:S(2)}, u32[]{:S(2)}) collective-permute-start(bf16[256,1024]{1,0:T(8,128)(2,1)} %collective-permute-done.5), channel_id=1, source_target_pairs={{0,4},{4,8},{8,12},{12,16},{16,20},{20,24},{24,28},{28,0},{1,5},{5... | collective-permute-start | bytes 1572872 | tf_op jit(solution)/shard_map/ppermute | solution.py:105
  678.9 105.0 %copy-start.9 = (f32[1024]{0:T(1024)S(1)}, f32[1024]{0:T(1024)}, u32[]{:S(2)}) copy-start(f32[1024]{0:T(1024)} %param.18) | copy-start | bytes 12292
  681.5 186.7 %copy-start.7 = (s32[1024]{0:T(1024)S(1)}, s32[1024]{0:T(1024)}, u32[]{:S(2)}) copy-start(s32[1024]{0:T(1024)} %param.19) | copy-start | bytes 12292
Sparse Core Ops, SparseCore 0:
  10.6 77.3 all-gather.3
  219.7 51.9 reduce-scatter.5
  275.3 146.8 reduce-scatter.3
  425.0 73.7 all-gather.5
  508.9 42.7 reduce-scatter.7
  681.6 102.2 all-gather.7
